TPU v7x, 32 devices: a whole 2x2x4 slice. The times are simulated.
32 devices in a mesh: end: 2 (over x), slab: 16 (over z, y, core).
Axes of the slice: x: 2, y: 2, z: 4, core: 2. Of those that a mesh axis runs over, the one named last changes fastest.
Arguments:
- w_field: float32 [128, 128, 256], P('slab'), may hold values from -4 to 4
- psi_init: float32 [128, 128, 256], P('slab'), may hold values from -3 to 3
- start_field: float32 [2, 128, 128, 256], P('end', 'slab'), may hold values from 0.25 to 8, as said below
- charges: int32 [5], replicated, may hold values from -1 to 1
Outputs:
- density: float32 [128, 128, 256], P('slab', 'end')
- potential: float32 [128, 128, 256], P('slab', 'end')
Inputs may be any that keep to these rules, and one draw needn't show every extreme that they name: `start_field`: positive entries.
All inputs are finite; a program needn't handle non-finite values.
Results may differ from a plain program's by a relative error of at most 0.0003.
The roundings to bfloat16 on the way count: a program that leaves them out, or rounds other values in their place, can miss the bound.
Values may be sent and summed in bfloat16 or wider, within the bound.
A program may use at most 64 MiB of HBM per device.

v0:
```python
import jax
import jax.numpy as jnp
from jax import lax
from jax.sharding import PartitionSpec as P

NS = 4
SWEEPS = 2


mobility = 0.15
screening = 1.0
crowding = 0.5


def padded_2(value, sides, width):
    for axis, dim in sides:
        size, length = (lax.axis_size(axis), value.shape[dim])
        up = [(i, (i + 1) % size) for i in range(size)]
        down = [(j, i) for i, j in up]
        last = lax.slice_in_dim(value, length - width, length, axis=dim)
        leading = lax.slice_in_dim(value, 0, width, axis=dim)
        before = lax.ppermute(last, axis, up)
        after = lax.ppermute(leading, axis, down)
        value = jnp.concatenate([before, value, after], axis=dim)
    return value


def swapped(block, axis, distance):
    count = lax.axis_size(axis)
    route = []
    for low in range(count):
        high = low | 1 << distance
        if high != low and high < count:
            route += [(low, high), (high, low)]
    return lax.ppermute(block, axis, route)


def ion_charge(value):
    return screening * jnp.sinh(value) / (1.0 + crowding * (jnp.cosh(value) - 1.0))


def relax(padded, charge):
    center = padded[1:-1, 1:-1]
    total = padded[2:, 1:-1] + padded[:-2, 1:-1] + padded[1:-1, 2:] + padded[1:-1, :-2]
    total = total + jnp.roll(center, 1, 2) + jnp.roll(center, -1, 2)
    return (total + charge - ion_charge(center) + screening * center) / (6.0 + screening)


def body(w_field, psi_init, start_field, charges):
    delta = 1.0 / NS
    side = lax.axis_index("end")
    valence = charges.astype(jnp.float32)
    current = start_field[0]
    history = [current]
    for layer in range(NS):
        contour = jnp.where(side == 0, layer, NS - 1 - layer)
        lower = lax.dynamic_index_in_dim(valence, contour, 0, False)
        upper = lax.dynamic_index_in_dim(valence, contour + 1, 0, False)
        factor = jnp.exp(-0.5 * delta * (w_field + 0.5 * (lower + upper) * psi_init))
        scaled = factor * current
        padded = padded_2(scaled, (("slab", 0),), 1)
        neighbours = padded[2:] + padded[:-2]
        neighbours = neighbours + jnp.roll(scaled, 1, 1) + jnp.roll(scaled, -1, 1)
        neighbours = neighbours + jnp.roll(scaled, 1, 2) + jnp.roll(scaled, -1, 2)
        current = factor * (scaled + mobility * (neighbours - 6.0 * scaled))
        history.append(current)
    ordered = jnp.stack(history)
    backward = jnp.stack(history[::-1])
    own = jnp.where(side == 0, ordered, backward).astype(jnp.bfloat16)
    weights = [delta * (0.5 if contour in (0, NS) else 1.0) for contour in range(NS + 1)]
    half_cells = own.shape[2] // lax.axis_size("end")
    keep = lax.dynamic_slice_in_dim(own, side * half_cells, half_cells, 2)
    send = lax.dynamic_slice_in_dim(own, (1 - side) * half_cells, half_cells, 2)
    partner = swapped(send, "end", 0)
    phi_half = jnp.zeros(keep.shape[1:], jnp.float32)
    rho_half = jnp.zeros(keep.shape[1:], jnp.float32)
    for contour in range(NS + 1):
        product = keep[contour].astype(jnp.float32) * partner[contour].astype(jnp.float32)
        phi_half = phi_half + weights[contour] * product
        rho_half = rho_half + weights[contour] * valence[contour] * product
    grand = lax.psum(jnp.sum(phi_half), ("end", "slab"))
    cells = phi_half.size * lax.axis_size("end") * lax.axis_size("slab")
    mean_total = grand / cells
    density = phi_half / mean_total
    charge = rho_half / mean_total
    potential = lax.dynamic_slice_in_dim(psi_init, side * half_cells, half_cells, 1)
    for sweep in range(SWEEPS):
        padded = padded_2(potential, (("end", 1), ("slab", 0)), 1)
        potential = relax(padded, charge)
    return (density, potential)


def solution(mesh):
    in_specs = (P("slab", None, None), P("slab", None, None), P("end", "slab", None, None), P())
    out_specs = (P("slab", "end", None), P("slab", "end", None))
    return jax.shard_map(body, mesh=mesh, in_specs=in_specs, out_specs=out_specs, check_vma=False)
```

profile of v0, /device:TPU:0, one launch (start us, length us, event | category | flops | bytes accessed | tf_op | source)
XLA Modules:
  0.0 145.9 jit_solution(3634529216103968016)
XLA Ops:
  0.6 0.7 convert_element_type.46
  1.3 0.7 fusion.92
  3.3 2.1 %bitcast_multiply_fusion = f32[8,128,256]{2,1,0:T(8,128)S(1)} fusion(f32[1,8,128,256]{3,2,1,0:T(8,128)} %param.6, f32[8,128,256]{2,1,0:T(8,128)} %param.4, f32[8,128,256]{2,1,0:T(8,128)} %param.5, f32[]{:T(128)} %bitcast), kind=kLoop, calls=%fused_computation.52 | loop fusion | flops 1048576 | bytes 4194308 | tf_op jit(solution)/shard_map/mul | solution.py:60
  5.4 0.7 fusion.84
  6.1 5.5 %collective-permute-start = (f32[1,128,256]{2,1,0:T(8,128)}, f32[1,128,256]{2,1,0:T(8,128)S(1)}, u32[]{:S(2)}, u32[]{:S(2)}) collective-permute-start(f32[1,128,256]{2,1,0:T(8,128)} %get-tuple-element.52), channel_id=1, source_target_pairs={{1,0},{2,1},{3,2},{4,3},{5,4},{6,5},{7,6},{8,7},{9,8},{10,9},{11,1... | collective-permute-start | bytes 393224 | tf_op jit(solution)/shard_map/ppermute | solution.py:23
  11.5 1.5 %fusion.86 = (f32[8,127,256]{2,1,0:T(8,128)}, f32[8,127,256]{2,1,0:T(8,128)}) fusion(f32[8,128,256]{2,1,0:T(8,128)S(1)} %bitcast_multiply_fusion), kind=kLoop, calls=%fused_computation.148 | loop fusion | bytes 4161536 | tf_op jit(solution)/shard_map/jit(_roll_static)/slice | solution.py:63
  13.1 1.7 %fusion.88 = (f32[8,128,255]{2,1,0:T(8,128)}, f32[8,128,255]{2,1,0:T(8,128)}) fusion(f32[8,128,256]{2,1,0:T(8,128)S(1)} %bitcast_multiply_fusion), kind=kLoop, calls=%fused_computation.150 | loop fusion | bytes 4177920 | tf_op jit(solution)/shard_map/jit(_roll_static)/slice | solution.py:64
  14.7 1.1 fusion.87
  19.7 0.0 collective-permute-done.1
  19.7 3.5 %fusion.61 = (f32[8,128,256]{2,1,0:T(8,128)S(1)}, bf16[8,128,256]{2,1,0:T(8,128)(2,1)S(1)}) fusion(f32[8,128,256]{2,1,0:T(8,128)S(1)} %copy-done.1, f32[8,128,256]{2,1,0:T(8,128)S(1)} %copy-done, f32[]{:T(128)} %bitcast.3, f32[8,128,256]{2,1,0:T(8,128)S(1)} %bitcast_multiply_fusion, f32[8,128,1]{2,1,0:T(8,128)} %get-tuple-element.59, ...), kind=kLoop, calls=%fused_computation.109 | loop fusion | flops 6291456 | bytes 9175048 | tf_op jit(solution)/shard_map/mul | solution.py:60
  23.2 0.2 fusion.81
  23.4 0.4 fusion.83
  23.8 0.2 fusion.82
  24.0 4.5 %collective-permute-start.2 = (f32[1,128,256]{2,1,0:T(8,128)S(1)}, f32[1,128,256]{2,1,0:T(8,128)S(1)}, u32[]{:S(2)}, u32[]{:S(2)}) collective-permute-start(f32[1,128,256]{2,1,0:T(8,128)S(1)} %get-tuple-element.42), channel_id=1, source_target_pairs={{1,0},{2,1},{3,2},{4,3},{5,4},{6,5},{7,6},{8,7},{9,8},{10,9},{11,1... | collective-permute-start | bytes 393224 | tf_op jit(solution)/shard_map/ppermute | solution.py:23
  28.5 0.0 collective-permute-start.3
  28.5 2.5 %collective-permute-done.2 = f32[1,128,256]{2,1,0:T(8,128)S(1)} collective-permute-done((f32[1,128,256]{2,1,0:T(8,128)S(1)}, f32[1,128,256]{2,1,0:T(8,128)S(1)}, u32[]{:S(2)}, u32[]{:S(2)}) %collective-permute-start.2) | collective-permute-done | bytes 131104 | tf_op jit(solution)/shard_map/ppermute | solution.py:23
  31.0 4.6 %collective-permute-done.3 = f32[1,128,256]{2,1,0:T(8,128)S(1)} collective-permute-done((f32[1,128,256]{2,1,0:T(8,128)S(1)}, f32[1,128,256]{2,1,0:T(8,128)S(1)}, u32[]{:S(2)}, u32[]{:S(2)}) %collective-permute-start.3) | collective-permute-done | bytes 131104 | tf_op jit(solution)/shard_map/ppermute | solution.py:22
  35.7 1.1 fusion.62
  36.8 0.2 fusion.76
  37.0 0.4 fusion.78
  37.3 0.2 fusion.77
  37.5 0.1 collective-permute-start.4
  37.6 0.5 collective-permute-start.5
  38.1 2.0 %collective-permute-done.4 = f32[1,128,256]{2,1,0:T(8,128)S(1)} collective-permute-done((f32[1,128,256]{2,1,0:T(8,128)S(1)}, f32[1,128,256]{2,1,0:T(8,128)S(1)}, u32[]{:S(2)}, u32[]{:S(2)}) %collective-permute-start.4) | collective-permute-done | bytes 131104 | tf_op jit(solution)/shard_map/ppermute | solution.py:23
  40.1 4.6 %collective-permute-done.5 = f32[1,128,256]{2,1,0:T(8,128)S(1)} collective-permute-done((f32[1,128,256]{2,1,0:T(8,128)S(1)}, f32[1,128,256]{2,1,0:T(8,128)S(1)}, u32[]{:S(2)}, u32[]{:S(2)}) %collective-permute-start.5) | collective-permute-done | bytes 131104 | tf_op jit(solution)/shard_map/ppermute | solution.py:22
  44.8 1.1 fusion.63
  45.9 0.2 fusion.71
  46.1 0.4 fusion.73
  46.4 0.2 fusion.72
  46.6 0.1 collective-permute-start.6
  46.7 0.5 collective-permute-start.7
  47.2 2.0 %collective-permute-done.6 = f32[1,128,256]{2,1,0:T(8,128)S(1)} collective-permute-done((f32[1,128,256]{2,1,0:T(8,128)S(1)}, f32[1,128,256]{2,1,0:T(8,128)S(1)}, u32[]{:S(2)}, u32[]{:S(2)}) %collective-permute-start.6) | collective-permute-done | bytes 131104 | tf_op jit(solution)/shard_map/ppermute | solution.py:23
  49.3 4.6 %collective-permute-done.7 = f32[1,128,256]{2,1,0:T(8,128)S(1)} collective-permute-done((f32[1,128,256]{2,1,0:T(8,128)S(1)}, f32[1,128,256]{2,1,0:T(8,128)S(1)}, u32[]{:S(2)}, u32[]{:S(2)}) %collective-permute-start.7) | collective-permute-done | bytes 131104 | tf_op jit(solution)/shard_map/ppermute | solution.py:22
  53.9 1.0 constant_dynamic-update-slice_fusion.3
  54.8 0.0 copy-start.3
  55.0 1.1 copy-done.3
  56.1 0.1 constant_dynamic-update-slice_fusion.2
  56.3 0.3 select_convert_fusion
  56.7 1.5 %copy-done.2 = bf16[5,8,128,256]{3,2,1,0:T(8,128)(2,1)} copy-done((bf16[5,8,128,256]{3,2,1,0:T(8,128)(2,1)}, bf16[5,8,128,256]{3,2,1,0:T(8,128)(2,1)S(1)}, u32[]{:S(2)}) %copy-start.2) | copy-done | bytes 2621464
  58.2 1.2 constant_dynamic-slice_fusion.7
  59.4 1.5 %collective-permute-start.8 = (bf16[5,8,64,256]{3,2,1,0:T(8,128)(2,1)}, bf16[5,8,64,256]{3,2,1,0:T(8,128)(2,1)S(1)}, u32[]{:S(2)}, u32[]{:S(2)}) collective-permute-start(bf16[5,8,64,256]{3,2,1,0:T(8,128)(2,1)} %constant_dynamic-slice_fusion.7), channel_id=1, source_target_pairs={{0,16},{16,0},{1,17},{17,1},{2,18},{18,2},{3,19},{19,3},{4,20},{20... | collective-permute-start | bytes 3932168 | tf_op jit(solution)/shard_map/ppermute | solution.py:35
  60.9 0.6 collective-permute-start.10
  61.5 1.5 %collective-permute-start.9 = (f32[8,1,256]{2,1,0:T(1,128)S(1)}, f32[8,1,256]{2,1,0:T(1,128)S(1)}, u32[]{:S(2)}, u32[]{:S(2)}) collective-permute-start(f32[8,1,256]{2,1,0:T(1,128)S(1)} %get-tuple-element.15), channel_id=1, source_target_pairs={{0,16},{16,0},{1,17},{17,1},{2,18},{18,2},{3,19},{19,3},{4,20},{20... | collective-permute-start | bytes 24584 | tf_op jit(solution)/shard_map/ppermute | solution.py:22
  63.0 1.1 constant_dynamic-slice_fusion.5
  64.2 0.9 constant_dynamic-slice_fusion
  68.1 17.7 %collective-permute-done.10 = f32[8,1,256]{2,1,0:T(1,128)S(1)} collective-permute-done((f32[8,1,256]{2,1,0:T(1,128)S(1)}, f32[8,1,256]{2,1,0:T(1,128)S(1)}, u32[]{:S(2)}, u32[]{:S(2)}) %collective-permute-start.10) | collective-permute-done | bytes 8224 | tf_op jit(solution)/shard_map/ppermute | solution.py:23
  85.8 0.1 collective-permute-done.9
  85.9 0.1 collective-permute-start.11
  86.0 0.5 collective-permute-start.12
  86.5 2.4 %fusion.64 = (f32[]{:T(128)}, f32[1,8,64,256]{3,2,1,0:T(8,128)S(1)}) fusion(bf16[5,8,64,256]{3,2,1,0:T(8,128)(2,1)S(1)} %collective-permute-done.8, bf16[5,8,128,256]{3,2,1,0:T(8,128)(2,1)} %copy-done.2, s32[]{:T(128)S(6)} %add.303, s32[]{:T(128)S(6)} %select_n.55, s32[]{:T(128)S(6)} %add.302, s32[]{:T(128)S(6)} %add.301, s32[]{:T(128)S(6)} %add.300), kind=kLoop, calls=%fused_computation.130 | loop fusion | flops 3276799 | bytes 3145752 | tf_op jit(solution)/shard_map/reduce_sum | solution.py:81
  88.9 38.7 %psum.7 = f32[]{:T(128)} all-reduce(f32[]{:T(128)} %get-tuple-element.4), channel_id=1, replica_groups=mesh['end'=2,'slab'=16] {'end','slab'}, use_global_device_ids=true, to_apply=%region_1.2 | all-reduce | flops 1 | bytes 8 | tf_op jit(solution)/shard_map/psum | solution.py:81
  128.3 3.1 %fusion.60 = (f32[8,64,256]{2,1,0:T(8,128)S(1)}, f32[1,8,64,256]{3,2,1,0:T(8,128)S(1)}) fusion(f32[8,64,256]{2,1,0:T(8,128)S(1)} %constant_dynamic-slice_fusion.6, f32[8,64,1]{2,1,0:T(8,128)} %get-tuple-element.17, f32[8,64,255]{2,1,0:T(8,128)} %get-tuple-element.19, f32[8,64,255]{2,1,0:T(8,128)} %get-tuple-element.18, f32[8,64,1]{2,1,0:T(8,128)} %get-tuple-element.16, ...), kind=kLoop, calls=%fused_computation.108 | loop fusion | flops 7733248 | bytes 5394476 | tf_op jit(solution)/shard_map/div | solution.py:46
  131.4 0.2 fusion.91
  131.6 2.3 %collective-permute-start.13 = (f32[8,1,256]{2,1,0:T(1,128)S(1)}, f32[8,1,256]{2,1,0:T(1,128)S(1)}, u32[]{:S(2)}, u32[]{:S(2)}) collective-permute-start(f32[8,1,256]{2,1,0:T(1,128)S(1)} %get-tuple-element.67), channel_id=1, source_target_pairs={{0,16},{16,0},{1,17},{17,1},{2,18},{18,2},{3,19},{19,3},{4,20},{20... | collective-permute-start | bytes 24584 | tf_op jit(solution)/shard_map/ppermute | solution.py:22
  133.9 0.1 collective-permute-start.14
  134.0 0.8 divide_bitcast_fusion
  134.9 0.7 collective-permute-done.13
  135.6 2.0 %collective-permute-done.14 = f32[8,1,256]{2,1,0:T(1,128)S(1)} collective-permute-done((f32[8,1,256]{2,1,0:T(1,128)S(1)}, f32[8,1,256]{2,1,0:T(1,128)S(1)}, u32[]{:S(2)}, u32[]{:S(2)}) %collective-permute-start.14) | collective-permute-done | bytes 8224 | tf_op jit(solution)/shard_map/ppermute | solution.py:23
  137.6 0.1 collective-permute-start.15
  137.7 0.5 collective-permute-start.16
  138.2 0.1 fusion.90
  138.3 1.3 collective-permute-done.15
  139.7 4.6 %collective-permute-done.16 = f32[1,66,256]{2,1,0:T(8,128)S(1)} collective-permute-done((f32[1,66,256]{2,1,0:T(8,128)S(1)}, f32[1,66,256]{2,1,0:T(8,128)S(1)}, u32[]{:S(2)}, u32[]{:S(2)}) %collective-permute-start.16) | collective-permute-done | bytes 67616 | tf_op jit(solution)/shard_map/ppermute | solution.py:22
  144.2 1.7 %fusion.59 = f32[8,64,256]{2,1,0:T(8,128)} fusion(f32[8,64,256]{2,1,0:T(8,128)S(1)} %get-tuple-element.2, f32[1,8,64,256]{3,2,1,0:T(8,128)S(1)} %get-tuple-element.3, f32[8,64,1]{2,1,0:T(8,128)S(1)} %get-tuple-element.69, f32[8,64,255]{2,1,0:T(8,128)S(1)} %get-tuple-element.71, f32[8,64,255]{2,1,0:T(8,128)S(1)} %get-tuple-element.70, ...), kind=kLoop, calls=%fused_computation.107 | loop fusion | flops 4456448 | bytes 2772992 | tf_op jit(solution)/shard_map/div | solution.py:46
  (33 shorter events, 0.5 us)
Async XLA Ops:
  6.1 13.6 %collective-permute-start = (f32[1,128,256]{2,1,0:T(8,128)}, f32[1,128,256]{2,1,0:T(8,128)S(1)}, u32[]{:S(2)}, u32[]{:S(2)}) collective-permute-start(f32[1,128,256]{2,1,0:T(8,128)} %get-tuple-element.52), channel_id=1, source_target_pairs={{1,0},{2,1},{3,2},{4,3},{5,4},{6,5},{7,6},{8,7},{9,8},{10,9},{11,1... | collective-permute-start | bytes 393224 | tf_op jit(solution)/shard_map/ppermute | solution.py:23
  11.5 8.1 %collective-permute-start.1 = (f32[1,128,256]{2,1,0:T(8,128)S(1)}, f32[1,128,256]{2,1,0:T(8,128)S(1)}, u32[]{:S(2)}, u32[]{:S(2)}) collective-permute-start(f32[1,128,256]{2,1,0:T(8,128)S(1)} %get-tuple-element.53), channel_id=1, source_target_pairs={{0,1},{1,2},{2,3},{3,4},{4,5},{5,6},{6,7},{7,8},{8,9},{9,10},{10,1... | collective-permute-start | bytes 393224 | tf_op jit(solution)/shard_map/ppermute | solution.py:22
  13.0 6.6 %copy-start = (f32[8,128,256]{2,1,0:T(8,128)S(1)}, f32[8,128,256]{2,1,0:T(8,128)}, u32[]{:S(2)}) copy-start(f32[8,128,256]{2,1,0:T(8,128)} %param.5) | copy-start | bytes 3145732
  13.1 6.6 %copy-start.1 = (f32[8,128,256]{2,1,0:T(8,128)S(1)}, f32[8,128,256]{2,1,0:T(8,128)}, u32[]{:S(2)}) copy-start(f32[8,128,256]{2,1,0:T(8,128)} %param.4) | copy-start | bytes 3145732
  24.0 7.0 %collective-permute-start.2 = (f32[1,128,256]{2,1,0:T(8,128)S(1)}, f32[1,128,256]{2,1,0:T(8,128)S(1)}, u32[]{:S(2)}, u32[]{:S(2)}) collective-permute-start(f32[1,128,256]{2,1,0:T(8,128)S(1)} %get-tuple-element.42), channel_id=1, source_target_pairs={{1,0},{2,1},{3,2},{4,3},{5,4},{6,5},{7,6},{8,7},{9,8},{10,9},{11,1... | collective-permute-start | bytes 393224 | tf_op jit(solution)/shard_map/ppermute | solution.py:23
  28.5 7.2 %collective-permute-start.3 = (f32[1,128,256]{2,1,0:T(8,128)S(1)}, f32[1,128,256]{2,1,0:T(8,128)S(1)}, u32[]{:S(2)}, u32[]{:S(2)}) collective-permute-start(f32[1,128,256]{2,1,0:T(8,128)S(1)} %get-tuple-element.43), channel_id=1, source_target_pairs={{0,1},{1,2},{2,3},{3,4},{4,5},{5,6},{6,7},{7,8},{8,9},{9,10},{10,1... | collective-permute-start | bytes 393224 | tf_op jit(solution)/shard_map/ppermute | solution.py:22
  37.5 2.6 %collective-permute-start.4 = (f32[1,128,256]{2,1,0:T(8,128)S(1)}, f32[1,128,256]{2,1,0:T(8,128)S(1)}, u32[]{:S(2)}, u32[]{:S(2)}) collective-permute-start(f32[1,128,256]{2,1,0:T(8,128)S(1)} %get-tuple-element.32), channel_id=1, source_target_pairs={{1,0},{2,1},{3,2},{4,3},{5,4},{6,5},{7,6},{8,7},{9,8},{10,9},{11,1... | collective-permute-start | bytes 393224 | tf_op jit(solution)/shard_map/ppermute | solution.py:23
  37.6 7.1 %collective-permute-start.5 = (f32[1,128,256]{2,1,0:T(8,128)S(1)}, f32[1,128,256]{2,1,0:T(8,128)S(1)}, u32[]{:S(2)}, u32[]{:S(2)}) collective-permute-start(f32[1,128,256]{2,1,0:T(8,128)S(1)} %get-tuple-element.33), channel_id=1, source_target_pairs={{0,1},{1,2},{2,3},{3,4},{4,5},{5,6},{6,7},{7,8},{8,9},{9,10},{10,1... | collective-permute-start | bytes 393224 | tf_op jit(solution)/shard_map/ppermute | solution.py:22
  46.6 2.6 %collective-permute-start.6 = (f32[1,128,256]{2,1,0:T(8,128)S(1)}, f32[1,128,256]{2,1,0:T(8,128)S(1)}, u32[]{:S(2)}, u32[]{:S(2)}) collective-permute-start(f32[1,128,256]{2,1,0:T(8,128)S(1)} %get-tuple-element.22), channel_id=1, source_target_pairs={{1,0},{2,1},{3,2},{4,3},{5,4},{6,5},{7,6},{8,7},{9,8},{10,9},{11,1... | collective-permute-start | bytes 393224 | tf_op jit(solution)/shard_map/ppermute | solution.py:23
  46.7 7.1 %collective-permute-start.7 = (f32[1,128,256]{2,1,0:T(8,128)S(1)}, f32[1,128,256]{2,1,0:T(8,128)S(1)}, u32[]{:S(2)}, u32[]{:S(2)}) collective-permute-start(f32[1,128,256]{2,1,0:T(8,128)S(1)} %get-tuple-element.23), channel_id=1, source_target_pairs={{0,1},{1,2},{2,3},{3,4},{4,5},{5,6},{6,7},{7,8},{8,9},{9,10},{10,1... | collective-permute-start | bytes 393224 | tf_op jit(solution)/shard_map/ppermute | solution.py:22
  54.8 1.2 copy-start.3
  56.7 1.5 %copy-start.2 = (bf16[5,8,128,256]{3,2,1,0:T(8,128)(2,1)}, bf16[5,8,128,256]{3,2,1,0:T(8,128)(2,1)S(1)}, u32[]{:S(2)}) copy-start(bf16[5,8,128,256]{3,2,1,0:T(8,128)(2,1)S(1)} %select_convert_fusion) | copy-start | bytes 7864324
  59.4 27.1 %collective-permute-start.8 = (bf16[5,8,64,256]{3,2,1,0:T(8,128)(2,1)}, bf16[5,8,64,256]{3,2,1,0:T(8,128)(2,1)S(1)}, u32[]{:S(2)}, u32[]{:S(2)}) collective-permute-start(bf16[5,8,64,256]{3,2,1,0:T(8,128)(2,1)} %constant_dynamic-slice_fusion.7), channel_id=1, source_target_pairs={{0,16},{16,0},{1,17},{17,1},{2,18},{18,2},{3,19},{19,3},{4,20},{20... | collective-permute-start | bytes 3932168 | tf_op jit(solution)/shard_map/ppermute | solution.py:35
  60.9 24.9 %collective-permute-start.10 = (f32[8,1,256]{2,1,0:T(1,128)S(1)}, f32[8,1,256]{2,1,0:T(1,128)S(1)}, u32[]{:S(2)}, u32[]{:S(2)}) collective-permute-start(f32[8,1,256]{2,1,0:T(1,128)S(1)} %get-tuple-element.14), channel_id=1, source_target_pairs={{16,0},{0,16},{17,1},{1,17},{18,2},{2,18},{19,3},{3,19},{20,4},{4,... | collective-permute-start | bytes 24584 | tf_op jit(solution)/shard_map/ppermute | solution.py:23
  61.5 24.4 %collective-permute-start.9 = (f32[8,1,256]{2,1,0:T(1,128)S(1)}, f32[8,1,256]{2,1,0:T(1,128)S(1)}, u32[]{:S(2)}, u32[]{:S(2)}) collective-permute-start(f32[8,1,256]{2,1,0:T(1,128)S(1)} %get-tuple-element.15), channel_id=1, source_target_pairs={{0,16},{16,0},{1,17},{17,1},{2,18},{18,2},{3,19},{19,3},{4,20},{20... | collective-permute-start | bytes 24584 | tf_op jit(solution)/shard_map/ppermute | solution.py:22
  85.8 0.7 copy-start.4
  85.9 0.6 copy-start.5
  85.9 42.3 %collective-permute-start.11 = (f32[1,66,256]{2,1,0:T(8,128)S(1)}, f32[1,66,256]{2,1,0:T(8,128)S(1)}, u32[]{:S(2)}, u32[]{:S(2)}) collective-permute-start(f32[1,66,256]{2,1,0:T(8,128)S(1)} %get-tuple-element.64), channel_id=1, source_target_pairs={{1,0},{2,1},{3,2},{4,3},{5,4},{6,5},{7,6},{8,7},{9,8},{10,9},{11,1... | collective-permute-start | bytes 202760 | tf_op jit(solution)/shard_map/ppermute | solution.py:23
  86.0 42.2 %collective-permute-start.12 = (f32[1,66,256]{2,1,0:T(8,128)S(1)}, f32[1,66,256]{2,1,0:T(8,128)S(1)}, u32[]{:S(2)}, u32[]{:S(2)}) collective-permute-start(f32[1,66,256]{2,1,0:T(8,128)S(1)} %get-tuple-element.65), channel_id=1, source_target_pairs={{0,1},{1,2},{2,3},{3,4},{4,5},{5,6},{6,7},{7,8},{8,9},{9,10},{10,1... | collective-permute-start | bytes 202760 | tf_op jit(solution)/shard_map/ppermute | solution.py:22
  131.6 4.0 %collective-permute-start.13 = (f32[8,1,256]{2,1,0:T(1,128)S(1)}, f32[8,1,256]{2,1,0:T(1,128)S(1)}, u32[]{:S(2)}, u32[]{:S(2)}) collective-permute-start(f32[8,1,256]{2,1,0:T(1,128)S(1)} %get-tuple-element.67), channel_id=1, source_target_pairs={{0,16},{16,0},{1,17},{17,1},{2,18},{18,2},{3,19},{19,3},{4,20},{20... | collective-permute-start | bytes 24584 | tf_op jit(solution)/shard_map/ppermute | solution.py:22
  133.9 3.7 %collective-permute-start.14 = (f32[8,1,256]{2,1,0:T(1,128)S(1)}, f32[8,1,256]{2,1,0:T(1,128)S(1)}, u32[]{:S(2)}, u32[]{:S(2)}) collective-permute-start(f32[8,1,256]{2,1,0:T(1,128)S(1)} %get-tuple-element.66), channel_id=1, source_target_pairs={{16,0},{0,16},{17,1},{1,17},{18,2},{2,18},{19,3},{3,19},{20,4},{4,... | collective-permute-start | bytes 24584 | tf_op jit(solution)/shard_map/ppermute | solution.py:23
  137.6 2.0 %collective-permute-start.15 = (f32[1,66,256]{2,1,0:T(8,128)S(1)}, f32[1,66,256]{2,1,0:T(8,128)S(1)}, u32[]{:S(2)}, u32[]{:S(2)}) collective-permute-start(f32[1,66,256]{2,1,0:T(8,128)S(1)} %get-tuple-element.62), channel_id=1, source_target_pairs={{1,0},{2,1},{3,2},{4,3},{5,4},{6,5},{7,6},{8,7},{9,8},{10,9},{11,1... | collective-permute-start | bytes 202760 | tf_op jit(solution)/shard_map/ppermute | solution.py:23
  137.7 6.5 %collective-permute-start.16 = (f32[1,66,256]{2,1,0:T(8,128)S(1)}, f32[1,66,256]{2,1,0:T(8,128)S(1)}, u32[]{:S(2)}, u32[]{:S(2)}) collective-permute-start(f32[1,66,256]{2,1,0:T(8,128)S(1)} %get-tuple-element.63), channel_id=1, source_target_pairs={{0,1},{1,2},{2,3},{3,4},{4,5},{5,6},{6,7},{7,8},{8,9},{9,10},{10,1... | collective-permute-start | bytes 202760 | tf_op jit(solution)/shard_map/ppermute | solution.py:22
where the time goes:
time: 146 us
  waiting for transfers between devices  46.8 us (32%)
  blocking collectives  38.7 us (27%)
  starting transfers between devices  18.2 us (12%)
  other arithmetic  17.8 us (12%)
  local copies, waits for them, and re-layouts  14.6 us (10%)
  between operations  9.77 us (7%)
    psum x1, blocking collectives, body(): grand = lax.psum(jnp.sum(phi_half), ('end', 'slab'))  38.7 us
    ppermute x8, waiting for transfers between devices, padded_2(): after = lax.ppermute(leading, axis, down)  27.6 us
    ppermute x8, waiting for transfers between devices, padded_2(): before = lax.ppermute(last, axis, up)  19.3 us
    ppermute x8, starting transfers between devices, padded_2(): after = lax.ppermute(leading, axis, down)  10.9 us
    mul x4, other arithmetic, body(): scaled = factor * current  7.79 us
    ppermute x8, starting transfers between devices, padded_2(): before = lax.ppermute(last, axis, up)  5.81 us
    div x2, other arithmetic, relax(): (total + charge - ion_charge(center) + screening * center) / (6.0 + scree...  4.75 us
    slice x8, local copies, waits for them, and re-layouts, body(): neighbours = neighbours + jnp.roll(scaled, 1, 2) + jnp.roll(scaled, -1, 2)  4.48 us
  transfers between devices with their start and end apart: 17, of which 12 were waited for; matrix products, arithmetic and copies ran while one was open for 7% of the time, Pallas kernels for 0%

commit v1 on v0

v1 whole, which is shorter than its diff:
```python
import functools

import jax
import jax.numpy as jnp
from jax import lax
from jax.experimental import pallas as pl
from jax.experimental.pallas import tpu as pltpu
from jax.sharding import PartitionSpec as P

NS = 4
PAD = 8
mobility = 0.15
screening = 1.0
OWN, FOREIGN = 0, 1
MESH = pl.DeviceIdType.MESH


def kernel(ends, slabs, charges_ref, w_hbm, psi_hbm, start_hbm, density_ref, potential_ref,
           w_v, psi_v, start_v, factor, u, rounded, phi, rho, base, relaxed, sums,
           local_sem, field_send, field_recv, psi_send, psi_recv, halo_send, halo_recv,
           rho_send, rho_recv, sum_send, sum_recv):
    side, slab = lax.axis_index("end"), lax.axis_index("slab")
    other = lax.rem(side + 1, ends)
    left = (side, lax.rem(slab + slabs - 1, slabs))
    right = (side, lax.rem(slab + 1, slabs))
    partner = (other, slab)
    layers, rows = w_hbm.shape[0], w_hbm.shape[1]
    half = rows // ends
    devices = ends * slabs
    flat = side * slabs + slab
    delta = 1.0 / NS

    def device(step):
        target = lax.rem(flat + step, devices)
        return (target // slabs, lax.rem(target, slabs))

    barrier = pltpu.get_barrier_semaphore()

    def greet(step, carry):
        pl.semaphore_signal(barrier, inc=1, device_id=device(step), device_id_type=MESH)
        return carry

    lax.fori_loop(1, devices, greet, 0)

    def pieces(which):
        first = which * half
        return (
            (pl.multiple_of(first, 8), PAD, half),
            (pl.multiple_of(lax.rem(first + rows - PAD, rows), 8), 0, PAD),
            (pl.multiple_of(lax.rem(first + half, rows), 8), PAD + half, PAD),
        )

    mine, theirs = pieces(side), pieces(other)
    local = []
    for k, (source, target, first) in enumerate(
        ((w_hbm, w_v, 0), (psi_hbm, psi_v, 2), (start_hbm.at[0], start_v.at[OWN], 0))
    ):
        for n, (begin, at, count) in enumerate(mine):
            local.append(
                pltpu.make_async_copy(
                    source.at[:, pl.ds(begin, count)],
                    target.at[pl.ds(first, layers), pl.ds(at, count)],
                    local_sem.at[k, n],
                )
            )
    for copy in local:
        copy.start()
    for copy in local:
        copy.wait()

    q = [charges_ref[side * (NS - 2 * t) + t].astype(jnp.float32) for t in range(NS + 1)]
    pair = [0.5 * (q[k] + q[k + 1]) for k in range(NS)]

    def make_factor(x, carry):
        w, psi = w_v[x], psi_v[x + 2]
        for k in range(NS):
            factor[k, x] = jnp.exp(-0.5 * delta * (w + pair[k] * psi))
        return carry

    def index(chain, t):
        return t if chain == OWN else NS - 1 - t

    def begin_chain(chain, x):
        value = start_v[chain, x]
        rounded[chain, 0, x] = value.astype(jnp.bfloat16).astype(jnp.float32)
        u[chain, 0, x + 1] = factor[index(chain, 0), x] * value

    def around(value, axis):
        return pltpu.roll(value, 1, axis) + pltpu.roll(value, value.shape[axis] - 1, axis)

    def advanced(chain, t, x):
        center = u[chain, t, x + 1]
        total = u[chain, t, x] + u[chain, t, x + 2] + around(center, 0) + around(center, 1)
        return factor[index(chain, t), x] * (center + mobility * (total - 6.0 * center))

    def advance(chain, t, x):
        value = advanced(chain, t, x)
        rounded[chain, t + 1, x] = value.astype(jnp.bfloat16).astype(jnp.float32)
        if t + 1 < NS:
            u[chain, t + 1, x + 1] = factor[index(chain, t + 1), x] * value

    def loop(low, high, step):
        def body(x, carry):
            step(x)
            return carry

        lax.fori_loop(low, high, body, 0)

    def both(step):
        step(0)
        step(layers - 1)

    def halo(chain, t):
        return (
            pltpu.make_async_remote_copy(
                u.at[chain, t, 1], u.at[chain, t, layers + 1],
                halo_send.at[chain, t, 0], halo_recv.at[chain, t, 0],
                device_id=left, device_id_type=MESH,
            ),
            pltpu.make_async_remote_copy(
                u.at[chain, t, layers], u.at[chain, t, 0],
                halo_send.at[chain, t, 1], halo_recv.at[chain, t, 1],
                device_id=right, device_id_type=MESH,
            ),
        )

    sent = []

    def send_halo(chain, t):
        for copy in halo(chain, t):
            copy.start()
            sent.append(copy)

    def wait_halo(chain, t):
        for copy in halo(chain, t):
            copy.wait_recv()

    groups = [(0, layers - 1), (1, layers - 2), (2, layers - 3), tuple(range(3, layers - 3))]
    order = [x for group in groups for x in group]

    def field(x):
        return [
            pltpu.make_async_remote_copy(
                start_hbm.at[0, x, pl.ds(begin, count)],
                start_v.at[FOREIGN, x, pl.ds(at, count)],
                field_send.at[x, n], field_recv.at[x, n],
                device_id=partner, device_id_type=MESH,
            )
            for n, (begin, at, count) in enumerate(theirs)
        ]

    def arrive(group):
        for x in groups[group]:
            for copy in field(x):
                copy.wait_recv()
        for x in groups[group]:
            begin_chain(FOREIGN, x)

    def psi_halo():
        copies = []
        for n, (begin, at, count) in enumerate(mine):
            copies.append(
                pltpu.make_async_remote_copy(
                    psi_hbm.at[pl.ds(0, 2), pl.ds(begin, count)],
                    psi_v.at[pl.ds(layers + 2, 2), pl.ds(at, count)],
                    psi_send.at[0, n], psi_recv.at[0, n],
                    device_id=left, device_id_type=MESH,
                )
            )
            copies.append(
                pltpu.make_async_remote_copy(
                    psi_hbm.at[pl.ds(layers - 2, 2), pl.ds(begin, count)],
                    psi_v.at[pl.ds(0, 2), pl.ds(at, count)],
                    psi_send.at[1, n], psi_recv.at[1, n],
                    device_id=right, device_id_type=MESH,
                )
            )
        return copies

    lax.fori_loop(0, layers, make_factor, 0)
    loop(0, layers, functools.partial(begin_chain, OWN))
    pl.semaphore_wait(barrier, devices - 1)

    for x in order:
        for copy in field(x):
            copy.start()
            sent.append(copy)
    send_halo(OWN, 0)
    psi_copies = psi_halo()
    for copy in psi_copies:
        copy.start()
        sent.append(copy)
    loop(1, layers - 1, functools.partial(advance, OWN, 0))

    arrive(0)
    send_halo(FOREIGN, 0)
    wait_halo(OWN, 0)
    both(functools.partial(advance, OWN, 0))
    send_halo(OWN, 1)
    loop(1, layers - 1, functools.partial(advance, OWN, 1))

    arrive(1)
    wait_halo(FOREIGN, 0)
    both(functools.partial(advance, FOREIGN, 0))
    send_halo(FOREIGN, 1)
    wait_halo(OWN, 1)
    both(functools.partial(advance, OWN, 1))
    send_halo(OWN, 2)
    loop(1, layers - 1, functools.partial(advance, OWN, 2))

    arrive(2)
    for x in (1, layers - 2):
        advance(FOREIGN, 0, x)
    wait_halo(FOREIGN, 1)
    both(functools.partial(advance, FOREIGN, 1))
    send_halo(FOREIGN, 2)
    wait_halo(OWN, 2)
    both(functools.partial(advance, OWN, 2))
    send_halo(OWN, 3)
    loop(1, layers - 1, functools.partial(advance, OWN, 3))

    arrive(3)
    loop(2, layers - 2, functools.partial(advance, FOREIGN, 0))
    loop(1, layers - 1, functools.partial(advance, FOREIGN, 1))
    wait_halo(FOREIGN, 2)
    both(functools.partial(advance, FOREIGN, 2))
    send_halo(FOREIGN, 3)
    loop(1, layers - 1, functools.partial(advance, FOREIGN, 2))
    wait_halo(OWN, 3)
    both(functools.partial(advance, OWN, 3))

    weights = [delta * (0.5 if t in (0, NS) else 1.0) for t in range(NS + 1)]
    charged = [weights[t] * q[t] for t in range(NS + 1)]

    def gather(x):
        phi_layer, rho_layer = 0.0, 0.0
        for t in range(1, NS + 1):
            product = rounded[OWN, t, x] * rounded[FOREIGN, NS - t, x]
            phi_layer = phi_layer + weights[t] * product
            rho_layer = rho_layer + charged[t] * product
        phi[x] = phi_layer
        rho[x + 1] = rho_layer

    def finish(x):
        value = advanced(FOREIGN, NS - 1, x).astype(jnp.bfloat16).astype(jnp.float32)
        product = rounded[OWN, 0, x] * value
        phi[x] += weights[0] * product
        rho[x + 1] += charged[0] * product

    loop(0, layers, gather)
    loop(1, layers - 1, finish)

    for copy in psi_copies:
        copy.wait_recv()

    def make_base(x):
        center = psi_v[x + 1]
        total = psi_v[x] + psi_v[x + 2] + around(center, 0) + around(center, 1)
        base[x] = total - ion_charge(center) + screening * center

    loop(0, layers + 2, make_base)

    wait_halo(FOREIGN, NS - 1)
    both(finish)
    rho_copies = (
        pltpu.make_async_remote_copy(
            rho.at[1], rho.at[layers + 1], rho_send.at[0], rho_recv.at[0],
            device_id=left, device_id_type=MESH,
        ),
        pltpu.make_async_remote_copy(
            rho.at[layers], rho.at[0], rho_send.at[1], rho_recv.at[1],
            device_id=right, device_id_type=MESH,
        ),
    )
    inner = pl.ds(PAD, half)

    def add(x, carry):
        return carry + phi[x, inner]

    partial = lax.fori_loop(1, layers, add, phi[0, inner])
    sums[0] = jnp.sum(
        sum(partial[:, k:k + 128] for k in range(0, partial.shape[1], 128)), axis=0, keepdims=True
    )

    def share(step, carry):
        pltpu.make_async_remote_copy(
            sums.at[0], sums.at[step], sum_send, sum_recv,
            device_id=device(step), device_id_type=MESH,
        ).start()
        return carry

    lax.fori_loop(1, devices, share, 0)
    for copy in rho_copies:
        copy.start()
        sent.append(copy)

    others = sums.at[pl.ds(1, devices - 1)]
    pltpu.make_async_copy(others, others, sum_recv).wait()
    cells = float(devices * layers * half * w_hbm.shape[2])
    inverse = cells / jnp.sum(sums[...])

    def relax_once(x):
        relaxed[x] = (base[x] + rho[x] * inverse) * (1.0 / (6.0 + screening))

    def first(x):
        density_ref[x] = phi[x, inner] * inverse
        relax_once(x + 1)

    loop(0, layers, first)

    def second(x):
        center = relaxed[x + 1]
        total = relaxed[x] + relaxed[x + 2] + around(center, 0) + around(center, 1)
        value = total + rho[x + 1] * inverse - ion_charge(center) + screening * center
        potential_ref[x] = value[PAD:PAD + half] * (1.0 / (6.0 + screening))

    loop(1, layers - 1, second)
    for copy in rho_copies:
        copy.wait_recv()
    relax_once(0)
    relax_once(layers + 1)
    both(second)

    for copy in sent:
        copy.wait_send()
    pltpu.make_async_copy(others, others, sum_send).wait()


def ion_charge(value):
    return (2.0 * screening) * jnp.tanh(0.5 * value)


def body(ends, slabs, w_field, psi_init, start_field, charges):
    layers, rows, depth = w_field.shape
    half = rows // ends
    wide = half + 2 * PAD
    devices = ends * slabs
    out = jax.ShapeDtypeStruct((layers, half, depth), jnp.float32)
    dma = pltpu.SemaphoreType.DMA

    def tile(*lead):
        return pltpu.VMEM((*lead, wide, depth), jnp.float32)

    hbm = pl.BlockSpec(memory_space=pl.ANY)
    vmem = pl.BlockSpec(memory_space=pltpu.VMEM)
    return pl.pallas_call(
        functools.partial(kernel, ends, slabs),
        out_shape=(out, out),
        in_specs=[pl.BlockSpec(memory_space=pltpu.SMEM), hbm, hbm, hbm],
        out_specs=(vmem, vmem),
        scratch_shapes=[
            tile(layers), tile(layers + 4), tile(2, layers), tile(NS, layers),
            tile(2, NS, layers + 2), tile(2, NS + 1, layers), tile(layers), tile(layers + 2),
            tile(layers + 2), tile(layers + 2), pltpu.VMEM((devices, 1, 128), jnp.float32),
            dma((3, 3)), dma((layers, 3)), dma((layers, 3)), dma((2, 3)), dma((2, 3)),
            dma((2, NS, 2)), dma((2, NS, 2)), dma((2,)), dma((2,)), dma(()), dma(()),
        ],
        compiler_params=pltpu.CompilerParams(
            collective_id=0, has_side_effects=True, vmem_limit_bytes=56 * 1024 * 1024
        ),
        name="scf_step",
    )(charges, w_field, psi_init, start_field)


def solution(mesh):
    in_specs = (P("slab", None, None), P("slab", None, None), P("end", "slab", None, None), P())
    out_specs = (P("slab", "end", None), P("slab", "end", None))
    step = functools.partial(body, mesh.shape["end"], mesh.shape["slab"])
    return jax.shard_map(step, mesh=mesh, in_specs=in_specs, out_specs=out_specs, check_vma=False)
```

time: 146 us -> 42.1 us (0.29)
  waiting for transfers between devices: 46.8 us -> 0 us
  blocking collectives: 38.7 us -> 0 us
  Pallas kernels: 0 us -> 38.6 us
  starting transfers between devices: 18.2 us -> 0 us
  other arithmetic: 17.8 us -> 0 us
  local copies, waits for them, and re-layouts: 14.6 us -> 2.72 us
  between operations: 9.77 us -> 0.65 us
    ppermute x17 -> x0, waiting for transfers between devices: 46.8 us -> none  [the longest x8 27.6 us: padded_2(): after = lax.ppermute(leading, axis, down)]
    psum x1 -> x0, blocking collectives: 38.7 us -> none  [body(): grand = lax.psum(jnp.sum(phi_half), ('end', 'slab'))]
    pallas_call x0 -> x1, Pallas kernels: none -> 38.6 us  [body(): pl.pallas_call(functools.partial(kernel, ends, slabs), out_shape=(out, ou...]
    ppermute x17 -> x0, starting transfers between devices: 18.2 us -> none  [the longest x8 10.9 us: padded_2(): after = lax.ppermute(leading, axis, down)]
    slice x27 -> x0, local copies, waits for them, and re-layouts: 10.4 us -> none  [the longest x8 4.48 us: body(): neighbours = neighbours + jnp.roll(scaled, 1, 2) + jnp.roll(scaled, -1, 2)]
    mul x4 -> x0, other arithmetic: 7.79 us -> none  [body(): scaled = factor * current]
    div x3 -> x0, other arithmetic: 5.6 us -> none  [the longest x2 4.75 us: relax(): (total + charge - ion_charge(center) + screening * center) / (6.0 + scree...]
    reduce_sum x1 -> x0, other arithmetic: 2.4 us -> none  [body(): grand = lax.psum(jnp.sum(phi_half), ('end', 'slab'))]
  transfers between devices with their start and end apart: 17 -> 0, of which waited for: 12 -> 0; matrix products, arithmetic and copies ran while one was open for 7% -> 0% of each run, Pallas kernels for 0% -> 0%
where the time goes in v1:
time: 42.1 us; the launch traced here: 41.9 us
  Pallas kernels  38.6 us (92%)
  local copies, waits for them, and re-layouts  2.72 us (6%)
  between operations  0.65 us (2%)
    pallas_call x1, Pallas kernels, body(): pl.pallas_call(functools.partial(kernel, ends, slabs), out_shape=(out, ou...  38.6 us
    unnamed x4, local copies, waits for them, and re-layouts  2.72 us

profile of v1, /device:TPU:0, one launch (start us, length us, event | category | flops | bytes accessed | tf_op | source)
XLA Modules:
  0.0 41.9 jit_solution(17733652860521184479)
XLA Ops:
  0.6 38.6 %scf_step.1 = (f32[8,64,256]{2,1,0:T(8,128)}, f32[8,64,256]{2,1,0:T(8,128)}) custom-call(s32[5]{0:T(128)} %charges_ref.1, f32[8,128,256]{2,1,0:T(8,128)} %w_hbm.1, f32[8,128,256]{2,1,0:T(8,128)} %psi_hbm.1, f32[1,8,128,256]{3,2,1,0:T(8,128)} %start_hbm.1), custom_call_target="tpu_custom_call" | custom-call | tf_op jit(solution)/shard_map/scf_step/pallas_call | solution.py:346
  39.2 0.0 copy-start
  39.2 1.9 %copy.8 = f32[8,64,256]{2,1,0:T(8,128)} copy(f32[8,64,256]{2,1,0:T(8,128)} %get-tuple-element.4) | data formatting | bytes 1048576
  41.1 0.0 copy-done
  41.1 0.8 %copy.9 = f32[8,64,256]{2,1,0:T(8,128)} copy(f32[8,64,256]{2,1,0:T(8,128)S(1)} %copy-done) | data formatting | bytes 1048576
Async XLA Ops:
  39.2 1.9 %copy-start = (f32[8,64,256]{2,1,0:T(8,128)S(1)}, f32[8,64,256]{2,1,0:T(8,128)}, u32[]{:S(2)}) copy-start(f32[8,64,256]{2,1,0:T(8,128)} %get-tuple-element.5) | copy-start | bytes 1572868

commit v2 on v1

--- a/solution.py
+++ b/solution.py
@@ -17,7 +17,7 @@
 
 def kernel(ends, slabs, charges_ref, w_hbm, psi_hbm, start_hbm, density_ref, potential_ref,
            w_v, psi_v, start_v, factor, u, rounded, phi, rho, base, relaxed, sums,
-           local_sem, field_send, field_recv, psi_send, psi_recv, halo_send, halo_recv,
+           gate, local_sem, field_send, field_recv, psi_send, psi_recv, halo_send, halo_recv,
            rho_send, rho_recv, sum_send, sum_recv):
     side, slab = lax.axis_index("end"), lax.axis_index("slab")
     other = lax.rem(side + 1, ends)
@@ -36,11 +36,14 @@
 
     barrier = pltpu.get_barrier_semaphore()
 
-    def greet(step, carry):
-        pl.semaphore_signal(barrier, inc=1, device_id=device(step), device_id_type=MESH)
-        return carry
-
-    lax.fori_loop(1, devices, greet, 0)
+    near = []
+    width = 1
+    while width < slabs:
+        near.append((side, slab + width - 2 * width * lax.rem(slab // width, 2)))
+        width *= 2
+    near.append(partner)
+    for neighbour in near:
+        pl.semaphore_signal(barrier, inc=1, device_id=neighbour, device_id_type=MESH)
 
     def pieces(which):
         first = which * half
@@ -65,8 +68,6 @@
             )
     for copy in local:
         copy.start()
-    for copy in local:
-        copy.wait()
 
     q = [charges_ref[side * (NS - 2 * t) + t].astype(jnp.float32) for t in range(NS + 1)]
     pair = [0.5 * (q[k] + q[k + 1]) for k in range(NS)]
@@ -177,14 +178,20 @@
             )
         return copies
 
-    lax.fori_loop(0, layers, make_factor, 0)
-    loop(0, layers, functools.partial(begin_chain, OWN))
-    pl.semaphore_wait(barrier, devices - 1)
-
+    pl.semaphore_wait(barrier, len(near))
     for x in order:
         for copy in field(x):
             copy.start()
             sent.append(copy)
+    for copy in local:
+        copy.wait()
+    stages = len(near)
+    for stage, neighbour in enumerate(near):
+        pl.semaphore_signal(gate.at[stage], inc=1, device_id=neighbour, device_id_type=MESH)
+        low, high = layers * stage // stages, layers * (stage + 1) // stages
+        lax.fori_loop(low, high, make_factor, 0)
+        loop(low, high, functools.partial(begin_chain, OWN))
+        pl.semaphore_wait(gate.at[stage], 1)
     send_halo(OWN, 0)
     psi_copies = psi_halo()
     for copy in psi_copies:
@@ -220,11 +227,15 @@
     loop(1, layers - 1, functools.partial(advance, OWN, 3))
 
     arrive(3)
-    loop(2, layers - 2, functools.partial(advance, FOREIGN, 0))
-    loop(1, layers - 1, functools.partial(advance, FOREIGN, 1))
+    for x in (2, layers - 3):
+        advance(FOREIGN, 0, x)
+    for x in (1, layers - 2):
+        advance(FOREIGN, 1, x)
     wait_halo(FOREIGN, 2)
     both(functools.partial(advance, FOREIGN, 2))
     send_halo(FOREIGN, 3)
+    loop(3, layers - 3, functools.partial(advance, FOREIGN, 0))
+    loop(2, layers - 2, functools.partial(advance, FOREIGN, 1))
     loop(1, layers - 1, functools.partial(advance, FOREIGN, 2))
     wait_halo(OWN, 3)
     both(functools.partial(advance, OWN, 3))
@@ -260,24 +271,25 @@
 
     loop(0, layers + 2, make_base)
 
+    inner = pl.ds(PAD, half)
+
+    def add(x, carry):
+        return carry + phi[x, inner]
+
+    partial = lax.fori_loop(2, layers - 1, add, phi[1, inner])
     wait_halo(FOREIGN, NS - 1)
     both(finish)
     rho_copies = (
         pltpu.make_async_remote_copy(
-            rho.at[1], rho.at[layers + 1], rho_send.at[0], rho_recv.at[0],
+            rho.at[1, inner], rho.at[layers + 1, inner], rho_send.at[0], rho_recv.at[0],
             device_id=left, device_id_type=MESH,
         ),
         pltpu.make_async_remote_copy(
-            rho.at[layers], rho.at[0], rho_send.at[1], rho_recv.at[1],
+            rho.at[layers, inner], rho.at[0, inner], rho_send.at[1], rho_recv.at[1],
             device_id=right, device_id_type=MESH,
         ),
     )
-    inner = pl.ds(PAD, half)
-
-    def add(x, carry):
-        return carry + phi[x, inner]
-
-    partial = lax.fori_loop(1, layers, add, phi[0, inner])
+    partial = partial + phi[0, inner] + phi[layers - 1, inner]
     sums[0] = jnp.sum(
         sum(partial[:, k:k + 128] for k in range(0, partial.shape[1], 128)), axis=0, keepdims=True
     )
@@ -335,13 +347,14 @@
     half = rows // ends
     wide = half + 2 * PAD
     devices = ends * slabs
+    stages = slabs.bit_length()
     out = jax.ShapeDtypeStruct((layers, half, depth), jnp.float32)
     dma = pltpu.SemaphoreType.DMA
 
     def tile(*lead):
         return pltpu.VMEM((*lead, wide, depth), jnp.float32)
 
-    hbm = pl.BlockSpec(memory_space=pl.ANY)
+    hbm = pl.BlockSpec(memory_space=pltpu.HBM)
     vmem = pl.BlockSpec(memory_space=pltpu.VMEM)
     return pl.pallas_call(
         functools.partial(kernel, ends, slabs),
@@ -352,11 +365,11 @@
             tile(layers), tile(layers + 4), tile(2, layers), tile(NS, layers),
             tile(2, NS, layers + 2), tile(2, NS + 1, layers), tile(layers), tile(layers + 2),
             tile(layers + 2), tile(layers + 2), pltpu.VMEM((devices, 1, 128), jnp.float32),
-            dma((3, 3)), dma((layers, 3)), dma((layers, 3)), dma((2, 3)), dma((2, 3)),
+            pltpu.SemaphoreType.REGULAR((stages,)), dma((3, 3)), dma((layers, 3)), dma((layers, 3)), dma((2, 3)), dma((2, 3)),
             dma((2, NS, 2)), dma((2, NS, 2)), dma((2,)), dma((2,)), dma(()), dma(()),
         ],
         compiler_params=pltpu.CompilerParams(
-            collective_id=0, has_side_effects=True, vmem_limit_bytes=56 * 1024 * 1024
+            collective_id=0, has_side_effects=True, vmem_limit_bytes=30 * 1024 * 1024
         ),
         name="scf_step",
     )(charges, w_field, psi_init, start_field)

time: 42.1 us -> 47.7 us (1.13)
  local copies, waits for them, and re-layouts: 2.72 us -> 5.91 us
  Pallas kernels: 38.6 us -> 40.9 us
    unnamed x4 -> x10, local copies, waits for them, and re-layouts: 2.72 us -> 5.91 us
    pallas_call x1, Pallas kernels: 38.6 us -> 40.9 us  [body(): pl.pallas_call(functools.partial(kernel, ends, slabs), out_shape=(out, ou...]
where the time goes in v2:
time: 47.7 us; the launch traced here: 47.5 us
  Pallas kernels  40.9 us (86%)
  local copies, waits for them, and re-layouts  5.91 us (12%)
  between operations  0.65 us (1%)
    pallas_call x1, Pallas kernels, body(): pl.pallas_call(functools.partial(kernel, ends, slabs), out_shape=(out, ou...  40.9 us
    unnamed x10, local copies, waits for them, and re-layouts  5.91 us

profile of v2, /device:TPU:0, one launch (start us, length us, event | category | flops | bytes accessed | tf_op | source)
XLA Modules:
  0.0 47.5 jit_solution(8490317681628114994)
XLA Ops:
  0.6 0.0 copy-start
  0.6 1.2 %copy-done = f32[8,128,256]{2,1,0:T(8,128)S(1)} copy-done((f32[8,128,256]{2,1,0:T(8,128)S(1)}, f32[8,128,256]{2,1,0:T(8,128)}, u32[]{:S(2)}) %copy-start) | copy-done | bytes 1048600
  1.9 0.0 copy-start.1
  1.9 1.2 %copy-done.1 = f32[8,128,256]{2,1,0:T(8,128)S(1)} copy-done((f32[8,128,256]{2,1,0:T(8,128)S(1)}, f32[8,128,256]{2,1,0:T(8,128)}, u32[]{:S(2)}) %copy-start.1) | copy-done | bytes 1048600
  3.1 0.0 copy-start.2
  3.1 1.2 %copy-done.2 = f32[1,8,128,256]{3,2,1,0:T(8,128)S(1)} copy-done((f32[1,8,128,256]{3,2,1,0:T(8,128)S(1)}, f32[1,8,128,256]{3,2,1,0:T(8,128)}, u32[]{:S(2)}) %copy-start.2) | copy-done | bytes 1048600
  4.3 0.0 copy-start.3
  4.3 0.7 %copy-done.3 = s32[5]{0:T(128)S(1)} copy-done((s32[5]{0:T(128)S(1)}, s32[5]{0:T(128)}, u32[]{:S(2)}) %copy-start.3) | copy-done | bytes 44
  5.0 40.9 %scf_step.1 = (f32[8,64,256]{2,1,0:T(8,128)S(1)}, f32[8,64,256]{2,1,0:T(8,128)S(1)}) custom-call(s32[5]{0:T(128)S(1)} %copy-done.3, f32[8,128,256]{2,1,0:T(8,128)S(1)} %copy-done, f32[8,128,256]{2,1,0:T(8,128)S(1)} %copy-done.1, f32[1,8,128,256]{3,2,1,0:T(8,128)S(1)} %copy-done.2), custom_call_target="tpu_custom_call" | custom-call | tf_op jit(solution)/shard_map/scf_step/pallas_call | solution.py:359
  45.9 0.8 %copy.8 = f32[8,64,256]{2,1,0:T(8,128)} copy(f32[8,64,256]{2,1,0:T(8,128)S(1)} %get-tuple-element.4) | data formatting | bytes 1048576
  46.7 0.8 %copy.9 = f32[8,64,256]{2,1,0:T(8,128)} copy(f32[8,64,256]{2,1,0:T(8,128)S(1)} %get-tuple-element.5) | data formatting | bytes 1048576
Async XLA Ops:
  0.6 1.2 %copy-start = (f32[8,128,256]{2,1,0:T(8,128)S(1)}, f32[8,128,256]{2,1,0:T(8,128)}, u32[]{:S(2)}) copy-start(f32[8,128,256]{2,1,0:T(8,128)} %w_hbm.1) | copy-start | bytes 3145732
  1.9 1.2 %copy-start.1 = (f32[8,128,256]{2,1,0:T(8,128)S(1)}, f32[8,128,256]{2,1,0:T(8,128)}, u32[]{:S(2)}) copy-start(f32[8,128,256]{2,1,0:T(8,128)} %psi_hbm.1) | copy-start | bytes 3145732
  3.1 1.2 %copy-start.2 = (f32[1,8,128,256]{3,2,1,0:T(8,128)S(1)}, f32[1,8,128,256]{3,2,1,0:T(8,128)}, u32[]{:S(2)}) copy-start(f32[1,8,128,256]{3,2,1,0:T(8,128)} %start_hbm.1) | copy-start | bytes 3145732
  4.3 0.7 %copy-start.3 = (s32[5]{0:T(128)S(1)}, s32[5]{0:T(128)}, u32[]{:S(2)}) copy-start(s32[5]{0:T(128)} %charges_ref.1) | copy-start | bytes 64

commit v3 on v2

--- a/solution.py
+++ b/solution.py
@@ -160,18 +160,19 @@
     def psi_halo():
         copies = []
         for n, (begin, at, count) in enumerate(mine):
+            deep = 2 if count == half else 1
             copies.append(
                 pltpu.make_async_remote_copy(
-                    psi_hbm.at[pl.ds(0, 2), pl.ds(begin, count)],
-                    psi_v.at[pl.ds(layers + 2, 2), pl.ds(at, count)],
+                    psi_hbm.at[pl.ds(0, deep), pl.ds(begin, count)],
+                    psi_v.at[pl.ds(layers + 2, deep), pl.ds(at, count)],
                     psi_send.at[0, n], psi_recv.at[0, n],
                     device_id=left, device_id_type=MESH,
                 )
             )
             copies.append(
                 pltpu.make_async_remote_copy(
-                    psi_hbm.at[pl.ds(layers - 2, 2), pl.ds(begin, count)],
-                    psi_v.at[pl.ds(0, 2), pl.ds(at, count)],
+                    psi_hbm.at[pl.ds(layers - deep, deep), pl.ds(begin, count)],
+                    psi_v.at[pl.ds(2 - deep, deep), pl.ds(at, count)],
                     psi_send.at[1, n], psi_recv.at[1, n],
                     device_id=right, device_id_type=MESH,
                 )
@@ -191,12 +192,9 @@
         low, high = layers * stage // stages, layers * (stage + 1) // stages
         lax.fori_loop(low, high, make_factor, 0)
         loop(low, high, functools.partial(begin_chain, OWN))
-        pl.semaphore_wait(gate.at[stage], 1)
+        if neighbour is not partner:
+            pl.semaphore_wait(gate.at[stage], 1)
     send_halo(OWN, 0)
-    psi_copies = psi_halo()
-    for copy in psi_copies:
-        copy.start()
-        sent.append(copy)
     loop(1, layers - 1, functools.partial(advance, OWN, 0))
 
     arrive(0)
@@ -234,6 +232,10 @@
     wait_halo(FOREIGN, 2)
     both(functools.partial(advance, FOREIGN, 2))
     send_halo(FOREIGN, 3)
+    psi_copies = psi_halo()
+    for copy in psi_copies:
+        copy.start()
+        sent.append(copy)
     loop(3, layers - 3, functools.partial(advance, FOREIGN, 0))
     loop(2, layers - 2, functools.partial(advance, FOREIGN, 1))
     loop(1, layers - 1, functools.partial(advance, FOREIGN, 2))
@@ -260,16 +262,6 @@
 
     loop(0, layers, gather)
     loop(1, layers - 1, finish)
-
-    for copy in psi_copies:
-        copy.wait_recv()
-
-    def make_base(x):
-        center = psi_v[x + 1]
-        total = psi_v[x] + psi_v[x + 2] + around(center, 0) + around(center, 1)
-        base[x] = total - ion_charge(center) + screening * center
-
-    loop(0, layers + 2, make_base)
 
     inner = pl.ds(PAD, half)
 
@@ -301,10 +293,21 @@
         ).start()
         return carry
 
+    pl.semaphore_wait(gate.at[stages - 1], 1)
     lax.fori_loop(1, devices, share, 0)
     for copy in rho_copies:
         copy.start()
         sent.append(copy)
+
+    for copy in psi_copies:
+        copy.wait_recv()
+
+    def make_base(x):
+        center = psi_v[x + 1]
+        total = psi_v[x] + psi_v[x + 2] + around(center, 0) + around(center, 1)
+        base[x] = total - ion_charge(center) + screening * center
+
+    loop(0, layers + 2, make_base)
 
     others = sums.at[pl.ds(1, devices - 1)]
     pltpu.make_async_copy(others, others, sum_recv).wait()
@@ -372,7 +375,7 @@
             collective_id=0, has_side_effects=True, vmem_limit_bytes=30 * 1024 * 1024
         ),
         name="scf_step",
-    )(charges, w_field, psi_init, start_field)
+    )(charges, *[pltpu.with_memory_space_constraint(v, pltpu.HBM) for v in (w_field, psi_init, start_field)])
 
 
 def solution(mesh):

time: 47.7 us -> 39.2 us (0.82)
  Pallas kernels: 40.9 us -> 36.2 us
  local copies, waits for them, and re-layouts: 5.91 us -> 2.24 us
    pallas_call x1, Pallas kernels: 40.9 us -> 36.2 us  [body(): pl.pallas_call(functools.partial(kernel, ends, slabs), out_shape=(out, ou...]
    unnamed x10 -> x4, local copies, waits for them, and re-layouts: 5.91 us -> 2.24 us
where the time goes in v3:
time: 39.2 us; the launch traced here: 39.1 us
  Pallas kernels  36.2 us (92%)
  local copies, waits for them, and re-layouts  2.24 us (6%)
  between operations  0.65 us (2%)
    pallas_call x1, Pallas kernels, body(): pl.pallas_call(functools.partial(kernel, ends, slabs), out_shape=(out, ou...  36.2 us
    unnamed x4, local copies, waits for them, and re-layouts  2.24 us

profile of v3, /device:TPU:0, one launch (start us, length us, event | category | flops | bytes accessed | tf_op | source)
XLA Modules:
  0.0 39.1 jit_solution(14682409397453094078)
XLA Ops:
  0.6 0.0 copy-start
  0.6 0.6 %copy-done = s32[5]{0:T(128)S(1)} copy-done((s32[5]{0:T(128)S(1)}, s32[5]{0:T(128)}, u32[]{:S(2)}) %copy-start) | copy-done | bytes 44
  1.3 36.2 %scf_step.1 = (f32[8,64,256]{2,1,0:T(8,128)S(1)}, f32[8,64,256]{2,1,0:T(8,128)S(1)}) custom-call(s32[5]{0:T(128)S(1)} %copy-done, f32[8,128,256]{2,1,0:T(8,128)} %w_hbm.1, f32[8,128,256]{2,1,0:T(8,128)} %psi_hbm.1, f32[1,8,128,256]{3,2,1,0:T(8,128)} %start_hbm.1), custom_call_target="tpu_custom_call" | custom-call | tf_op jit(solution)/shard_map/scf_step/pallas_call | solution.py:362
  37.5 0.8 %copy.8 = f32[8,64,256]{2,1,0:T(8,128)} copy(f32[8,64,256]{2,1,0:T(8,128)S(1)} %get-tuple-element.4) | data formatting | bytes 1048576
  38.3 0.8 %copy.9 = f32[8,64,256]{2,1,0:T(8,128)} copy(f32[8,64,256]{2,1,0:T(8,128)S(1)} %get-tuple-element.5) | data formatting | bytes 1048576
Async XLA Ops:
  0.6 0.7 %copy-start = (s32[5]{0:T(128)S(1)}, s32[5]{0:T(128)}, u32[]{:S(2)}) copy-start(s32[5]{0:T(128)} %charges_ref.1) | copy-start | bytes 64

commit v4 on v3

--- a/solution.py
+++ b/solution.py
@@ -197,6 +197,13 @@
     send_halo(OWN, 0)
     loop(1, layers - 1, functools.partial(advance, OWN, 0))
 
+    def make_base(x):
+        center = psi_v[x + 1]
+        total = psi_v[x] + psi_v[x + 2] + around(center, 0) + around(center, 1)
+        base[x] = total - ion_charge(center) + screening * center
+
+    loop(2, layers, make_base)
+
     arrive(0)
     send_halo(FOREIGN, 0)
     wait_halo(OWN, 0)
@@ -245,23 +252,34 @@
     weights = [delta * (0.5 if t in (0, NS) else 1.0) for t in range(NS + 1)]
     charged = [weights[t] * q[t] for t in range(NS + 1)]
 
-    def gather(x):
+    def gathered(x):
         phi_layer, rho_layer = 0.0, 0.0
         for t in range(1, NS + 1):
             product = rounded[OWN, t, x] * rounded[FOREIGN, NS - t, x]
             phi_layer = phi_layer + weights[t] * product
             rho_layer = rho_layer + charged[t] * product
-        phi[x] = phi_layer
-        rho[x + 1] = rho_layer
+        return phi_layer, rho_layer
+
+    def gather(x):
+        phi[x], rho[x + 1] = gathered(x)
+
+    def last_product(x):
+        value = advanced(FOREIGN, NS - 1, x).astype(jnp.bfloat16).astype(jnp.float32)
+        return rounded[OWN, 0, x] * value
 
     def finish(x):
-        value = advanced(FOREIGN, NS - 1, x).astype(jnp.bfloat16).astype(jnp.float32)
-        product = rounded[OWN, 0, x] * value
+        product = last_product(x)
         phi[x] += weights[0] * product
         rho[x + 1] += charged[0] * product
 
-    loop(0, layers, gather)
-    loop(1, layers - 1, finish)
+    def whole(x):
+        phi_layer, rho_layer = gathered(x)
+        product = last_product(x)
+        phi[x] = phi_layer + weights[0] * product
+        rho[x + 1] = rho_layer + charged[0] * product
+
+    both(gather)
+    loop(1, layers - 1, whole)
 
     inner = pl.ds(PAD, half)
 
@@ -302,12 +320,8 @@
     for copy in psi_copies:
         copy.wait_recv()
 
-    def make_base(x):
-        center = psi_v[x + 1]
-        total = psi_v[x] + psi_v[x + 2] + around(center, 0) + around(center, 1)
-        base[x] = total - ion_charge(center) + screening * center
-
-    loop(0, layers + 2, make_base)
+    for x in (0, 1, layers, layers + 1):
+        make_base(x)
 
     others = sums.at[pl.ds(1, devices - 1)]
     pltpu.make_async_copy(others, others, sum_recv).wait()

time: 39.2 us -> 38.9 us (level)
  no operation moved by 1% of the time
where the time goes in v4:
time: 38.9 us; the launch traced here: 38.8 us
  Pallas kernels  35.9 us (92%)
  local copies, waits for them, and re-layouts  2.24 us (6%)
  between operations  0.65 us (2%)
    pallas_call x1, Pallas kernels, body(): pl.pallas_call(functools.partial(kernel, ends, slabs), out_shape=(out, ou...  35.9 us
    unnamed x4, local copies, waits for them, and re-layouts  2.24 us

profile of v4, /device:TPU:0, one launch (start us, length us, event | category | flops | bytes accessed | tf_op | source)
XLA Modules:
  0.0 38.8 jit_solution(11590226411625054319)
XLA Ops:
  0.6 0.0 copy-start
  0.6 0.6 %copy-done = s32[5]{0:T(128)S(1)} copy-done((s32[5]{0:T(128)S(1)}, s32[5]{0:T(128)}, u32[]{:S(2)}) %copy-start) | copy-done | bytes 44
  1.3 35.9 %scf_step.1 = (f32[8,64,256]{2,1,0:T(8,128)S(1)}, f32[8,64,256]{2,1,0:T(8,128)S(1)}) custom-call(s32[5]{0:T(128)S(1)} %copy-done, f32[8,128,256]{2,1,0:T(8,128)} %w_hbm.1, f32[8,128,256]{2,1,0:T(8,128)} %psi_hbm.1, f32[1,8,128,256]{3,2,1,0:T(8,128)} %start_hbm.1), custom_call_target="tpu_custom_call" | custom-call | tf_op jit(solution)/shard_map/scf_step/pallas_call | solution.py:376
  37.2 0.8 %copy.8 = f32[8,64,256]{2,1,0:T(8,128)} copy(f32[8,64,256]{2,1,0:T(8,128)S(1)} %get-tuple-element.4) | data formatting | bytes 1048576
  38.0 0.8 %copy.9 = f32[8,64,256]{2,1,0:T(8,128)} copy(f32[8,64,256]{2,1,0:T(8,128)S(1)} %get-tuple-element.5) | data formatting | bytes 1048576
Async XLA Ops:
  0.6 0.7 %copy-start = (s32[5]{0:T(128)S(1)}, s32[5]{0:T(128)}, u32[]{:S(2)}) copy-start(s32[5]{0:T(128)} %charges_ref.1) | copy-start | bytes 64
